TPU v7x, 128 devices: a whole 4x4x4 slice. The times are simulated.
128 devices in a mesh: group: 4 (over z), shard: 32 (over x, y, core).
Axes of the slice: x: 4, y: 4, z: 4, core: 2. Of those that a mesh axis runs over, the one named last changes fastest.
Arguments:
- vectors: float32 [16384, 256], P(('group', 'shard')), may hold values from -160 to 160
- item_codes: int32 [16384], P(('group', 'shard')), may hold values from 0 to 63, as said below
- coarse_book: float32 [64, 256], replicated, may hold values from -24 to 24
- fine_books: float32 [8, 16384, 256], P('group', 'shard'), may hold values from -2 to 2
Outputs:
- item_grad: float32 [16384, 256], P(('group', 'shard'))
- fine_grad: float32 [8, 16384, 256], P('group', 'shard')
- coarse_grad: float32 [64, 256], replicated
Inputs may be any that keep to these rules, and one draw needn't show every extreme that they name: `item_codes`: the items of one device fall into one group at most 32 times, and one group receives exactly 32 items from every device.
All inputs are finite; a program needn't handle non-finite values.
Results may differ from a plain program's by a relative error of at most 0.0003.
Values sent between devices are 32-bit elements; how exact they have to be, the bound alone decides.
No kernel may reach another device: no remote copies, remote signals or barrier semaphores. Data moves between devices by JAX's collectives and lax.ppermute only.
A program may use at most 192 MiB of HBM per device.

v0:
```python
import jax
import jax.numpy as jnp
from jax import lax
from jax.sharding import PartitionSpec as P

sharpness = 2.5
highest = lax.Precision.HIGHEST


def contract(former, latter, former_dim, latter_dim):
    return lax.dot_general(
        former,
        latter,
        (((former_dim,), (latter_dim,)), ((), ())),
        precision=highest,
        preferred_element_type=jnp.float32,
    )


def per_device(vectors, item_codes, coarse_book, fine_books):
    local_groups, book_rows, feature_count = fine_books.shape
    group_count = lax.axis_size("group")
    total_groups = local_groups * group_count
    coarse_total = coarse_book.shape[0]
    per_group = coarse_total // total_groups
    item_count = vectors.shape[0]
    slot_size = item_count // 4
    slot_total = local_groups * group_count * slot_size
    onehot = (item_codes[:, None] == jnp.arange(coarse_total, dtype=jnp.int32)[None, :]).astype(
        jnp.float32
    )
    residual = vectors - contract(onehot, coarse_book, 1, 0)
    group_of = item_codes // per_group
    member = (group_of[:, None] == jnp.arange(total_groups, dtype=jnp.int32)[None, :]).astype(
        jnp.int32
    )
    position = jnp.sum((jnp.cumsum(member, axis=0) - 1) * member, axis=1)
    target = (
        group_of % local_groups * group_count + group_of // local_groups
    ) * slot_size + position
    placing = (jnp.arange(slot_total, dtype=jnp.int32)[:, None] == target[None, :]).astype(
        jnp.float32
    )
    outgoing = contract(placing, residual, 1, 0).reshape(
        local_groups, group_count, slot_size, feature_count
    )
    occupied = jnp.sum(placing, axis=1).reshape(local_groups, group_count, slot_size)
    arrived, arrived_mask = (
        lax.all_to_all(outgoing, "group", split_axis=1, concat_axis=1, tiled=True),
        lax.all_to_all(occupied, "group", split_axis=1, concat_axis=1, tiled=True),
    )
    own_count = group_count * slot_size
    own_rows = arrived.reshape(local_groups, own_count, feature_count)
    own_live = arrived_mask.reshape(local_groups, own_count)
    row_grads = []
    book_grads = []
    spread_rows, spread_mask = (
        lax.all_gather(arrived, "shard", axis=1, tiled=True),
        lax.all_gather(arrived_mask, "shard", axis=1, tiled=True),
    )
    row_total = spread_rows.shape[1] * slot_size
    all_rows = spread_rows.reshape(local_groups, row_total, feature_count)
    for book_index in range(local_groups):
        codebook = fine_books[book_index]
        entries = all_rows[book_index]
        scores = sharpness * contract(entries, codebook, 1, 1)
        peak_score = lax.pmax(jnp.max(scores, axis=1), "shard")
        weights = jnp.exp(scores - peak_score[:, None])
        partial_total = jnp.sum(weights, axis=1)
        partial_quant = contract(weights, codebook, 1, 0)
        quant_sum, denominator_own = (
            lax.psum_scatter(partial_quant, "shard", scatter_dimension=0, tiled=True),
            lax.psum_scatter(partial_total, "shard", scatter_dimension=0, tiled=True),
        )
        quantized = quant_sum / denominator_own[:, None]
        own_error = (quantized - own_rows[book_index]) * own_live[book_index][:, None]
        own_inner = jnp.sum(own_error * quantized, axis=1)
        error_rows, inner_term, denominator = (
            lax.all_gather(own_error, "shard", axis=0, tiled=True),
            lax.all_gather(own_inner, "shard", axis=0, tiled=True),
            lax.all_gather(denominator_own, "shard", axis=0, tiled=True),
        )
        probability = weights / denominator[:, None]
        alignment = contract(error_rows, codebook, 1, 1)
        slopes = probability * (alignment - inner_term[:, None])
        pushed = sharpness * contract(slopes, codebook, 1, 0)
        back_sum = lax.psum_scatter(pushed, "shard", scatter_dimension=0, tiled=True)
        row_grads.append(back_sum - own_error)
        book_grads.append(
            contract(probability, error_rows, 0, 0) + sharpness * contract(slopes, entries, 0, 0)
        )
    fine_grad = jnp.stack(book_grads)
    returned = jnp.stack(row_grads).reshape(local_groups, group_count, slot_size, feature_count)
    homeward = lax.all_to_all(returned, "group", split_axis=1, concat_axis=1, tiled=True)
    item_grad = contract(placing, homeward.reshape(slot_total, feature_count), 0, 0)
    coarse_grad = lax.psum(-contract(onehot, item_grad, 0, 0), ("group", "shard"))
    return (item_grad, fine_grad, coarse_grad)


def solution(mesh):
    placed = (P(("group", "shard"), None), P(("group", "shard")), P(), P("group", "shard", None))
    return jax.shard_map(
        per_device,
        mesh=mesh,
        in_specs=placed,
        out_specs=(P(("group", "shard"), None), P("group", "shard", None), P()),
        check_vma=False,
    )
```

profile of v0, /device:TPU:1, one launch (start us, length us, event | category | flops | bytes accessed | tf_op | source)
XLA Modules:
  0.0 839.8 jit_solution(5621896040765602508)
XLA Ops:
  7.2 0.7 and_select_fusion.2
  8.3 0.7 multiply_add_fusion
  9.0 1.2 convolution_subtract_fusion
  10.2 0.3 fusion.47
  10.5 11.3 %all_to_all.15 = f32[2,4,32,256]{3,2,0,1:T(8,128)} all-to-all(f32[2,4,32,256]{3,2,0,1:T(8,128)S(1)} %copy.28), channel_id=1, replica_groups=mesh['group'=4,'shard'=32] {'group'}, dimensions={1} | all-to-all | bytes 524288 | tf_op jit(solution)/shard_map/all_to_all | solution.py:49
  21.9 54.1 %all-gather.8.cloned.1.call-done = f32[2,128,32,256]{3,2,0,1:T(8,128)} async-done(((f32[2,4,32,256]{3,2,0,1:T(8,128)}), f32[2,128,32,256]{3,2,0,1:T(8,128)}) %all-gather.8.cloned.1.call-update) | async-done | bytes 8388624 | tf_op jit(solution)/shard_map/all_gather | solution.py:58
  76.0 4.4 fusion.61
  80.4 9.2 %multiply_reduce_fusion = (f32[4096]{0:T(1024)S(1)}, f32[4096,512]{0,1:T(8,128)}) fusion(f32[4096,256]{1,0:T(8,128)S(1)} %bitcast.75, f32[2,512,256]{2,1,0:T(8,128)S(1)} %copy-done.8), kind=kOutput, calls=%fused_computation.4 | convolution fusion | flops 6446641152 | bytes 13123584 | tf_op jit(solution)/shard_map/dot_general | solution.py:11
  89.6 9.2 %multiply_reduce_fusion.1 = (f32[4096]{0:T(1024)S(1)}, f32[4096,512]{0,1:T(8,128)}) fusion(f32[4096,256]{1,0:T(8,128)S(1)} %bitcast.77, f32[2,512,256]{2,1,0:T(8,128)S(1)} %copy-done.8), kind=kOutput, calls=%fused_computation.5 | convolution fusion | flops 6446641152 | bytes 13123584 | tf_op jit(solution)/shard_map/dot_general | solution.py:11
  98.8 121.3 %all-reduce.3 = (f32[4096]{0:T(1024)S(1)}, f32[4096]{0:T(1024)S(1)}) all-reduce(f32[4096]{0:T(1024)S(1)} %get-tuple-element.17, f32[4096]{0:T(1024)S(1)} %get-tuple-element.19), channel_id=1, replica_groups=mesh['group'=4,'shard'=32] {'shard'}, use_global_device_ids=true, to_apply=%region_11.12 | all-reduce | flops 8192 | bytes 65536 | tf_op jit(solution)/shard_map/pmax | solution.py:67
  220.2 17.2 %fusion = f32[4096,256]{1,0:T(8,128)} fusion(f32[4096,512]{0,1:T(8,128)} %get-tuple-element.20, f32[4096]{0:T(1024)S(1)} %get-tuple-element.8, f32[2,512,256]{2,1,0:T(8,128)S(1)} %copy-done.8), kind=kOutput, calls=%fused_computation.8 | convolution fusion | flops 6446645248 | bytes 13123584 | tf_op jit(solution)/shard_map/dot_general | solution.py:11
  237.6 17.2 %fusion.3 = f32[4096,256]{1,0:T(8,128)} fusion(f32[4096,512]{0,1:T(8,128)} %get-tuple-element.18, f32[4096]{0:T(1024)S(1)} %get-tuple-element.7, f32[2,512,256]{2,1,0:T(8,128)S(1)} %copy-done.8), kind=kOutput, calls=%fused_computation.11 | convolution fusion | flops 6446645248 | bytes 13123584 | tf_op jit(solution)/shard_map/dot_general | solution.py:11
  255.0 0.6 copy.29
  255.7 4.1 all-to-all-start.1
  259.8 0.6 dynamic-slice
  261.0 2.9 all-to-all-done.1
  264.1 5.0 fusion.2
  269.1 5.0 fusion.5
  274.1 125.5 %all-reduce.2 = (f32[4096]{0:T(1024)S(1)}, f32[4096]{0:T(1024)S(1)}) all-reduce(f32[4096]{0:T(1024)S(1)} %fusion.5, f32[4096]{0:T(1024)S(1)} %fusion.2), channel_id=5, replica_groups=mesh['group'=4,'shard'=32] {'shard'}, use_global_device_ids=true, to_apply=%region_13.14.clone | all-reduce | flops 8192 | bytes 65536
  399.7 1.7 multiply_reduce_fusion.3
  401.6 3.3 reduce-scatter.9.cloned.1.call-done
  404.9 1.7 multiply_reduce_fusion.2
  406.8 22.6 %all-gather = f32[32,1,128]{2,1,0:T(1,128)S(1)} all-gather(f32[1,1,128]{2,1,0:T(1,128)S(1)} %dynamic-slice_bitcast_fusion), channel_id=1, replica_groups=mesh['group'=4,'shard'=32] {'shard'}, dimensions={0}, use_global_device_ids=true | all-gather | bytes 16896 | tf_op jit(solution)/shard_map/all_gather | solution.py:81
  429.3 20.8 %all-gather.1 = f32[32,1,128]{2,1,0:T(1,128)S(1)} all-gather(f32[1,1,128]{2,1,0:T(1,128)S(1)} %bitcast.89), channel_id=1, replica_groups=mesh['group'=4,'shard'=32] {'shard'}, dimensions={0}, use_global_device_ids=true | all-gather | bytes 16896 | tf_op jit(solution)/shard_map/all_gather | solution.py:80
  450.1 4.9 all-gather.10.cloned.1.call-done
  455.0 12.0 %subtract_multiply_fusion.1 = f32[4096,512]{0,1:T(8,128)S(1)} fusion(f32[4096,256]{1,0:T(8,128)} %all-gather.10.cloned.1.call-done, f32[4096]{0:T(1024)S(1)} %bitcast.87, f32[4096]{0:T(1024)S(1)} %bitcast.85, f32[4096]{0:T(1024)S(1)} %get-tuple-element.8, f32[4096,512]{0,1:T(8,128)} %get-tuple-element.20, f32[2,512,256]{2,1,0:T(8,128)S(1)} %copy-done.8), kind=kOutput, calls=%fused_computation.2 | convolution fusion | flops 6452936704 | bytes 21544960 | tf_op jit(solution)/shard_map/dot_general | solution.py:11
  467.0 3.2 copy-done.2
  470.2 15.4 %convolution_multiply_fusion.1 = f32[4096,256]{1,0:T(8,128)} fusion(f32[4096,512]{0,1:T(8,128)S(1)} %subtract_multiply_fusion.1, f32[2,512,256]{2,1,0:T(8,128)S(1)} %copy-done.8), kind=kOutput, calls=%fused_computation.7 | convolution fusion | flops 6443499520 | bytes 13107200 | tf_op jit(solution)/shard_map/dot_general | solution.py:11
  485.8 20.6 %all-gather.2 = f32[32,1,128]{2,1,0:T(1,128)S(1)} all-gather(f32[1,1,128]{2,1,0:T(1,128)S(1)} %dynamic-slice_bitcast_fusion.1), channel_id=1, replica_groups=mesh['group'=4,'shard'=32] {'shard'}, dimensions={0}, use_global_device_ids=true | all-gather | bytes 16896 | tf_op jit(solution)/shard_map/all_gather | solution.py:81
  506.4 19.8 %all-gather.3 = f32[32,1,128]{2,1,0:T(1,128)S(1)} all-gather(f32[1,1,128]{2,1,0:T(1,128)S(1)} %bitcast.90), channel_id=1, replica_groups=mesh['group'=4,'shard'=32] {'shard'}, dimensions={0}, use_global_device_ids=true | all-gather | bytes 16896 | tf_op jit(solution)/shard_map/all_gather | solution.py:80
  526.2 12.2 %subtract_multiply_fusion = f32[4096,512]{0,1:T(8,128)S(1)} fusion(f32[4096,256]{1,0:T(8,128)} %all-gather.12.cloned.1.call-done, f32[4096]{0:T(1024)S(1)} %bitcast.88, f32[4096]{0:T(1024)S(1)} %bitcast.83, f32[4096]{0:T(1024)S(1)} %get-tuple-element.7, f32[4096,512]{0,1:T(8,128)} %get-tuple-element.18, f32[2,512,256]{2,1,0:T(8,128)S(1)} %copy-done.8), kind=kOutput, calls=%fused_computation | convolution fusion | flops 6452936704 | bytes 21544960 | tf_op jit(solution)/shard_map/dot_general | solution.py:11
  538.4 3.2 copy-done.3
  541.6 15.4 %convolution_multiply_fusion = f32[4096,256]{1,0:T(8,128)} fusion(f32[4096,512]{0,1:T(8,128)S(1)} %subtract_multiply_fusion, f32[2,512,256]{2,1,0:T(8,128)S(1)} %copy-done.8), kind=kOutput, calls=%fused_computation.6 | convolution fusion | flops 6443499520 | bytes 13107200 | tf_op jit(solution)/shard_map/dot_general | solution.py:11
  557.0 10.3 %convolution_multiply_fusion.3 = f32[512,256]{1,0:T(8,128)S(1)} fusion(f32[4096,512]{0,1:T(8,128)} %copy-done.2, f32[4096,256]{1,0:T(8,128)} %bitcast.78), kind=kOutput, calls=%fused_computation.21 | convolution fusion | flops 6442582016 | bytes 13107200 | tf_op jit(solution)/shard_map/dot_general | solution.py:11
  567.4 6.7 convolution_multiply_fusion.2
  574.1 8.1 fusion.17
  582.2 3.8 reduce-scatter.7.cloned.1.call-done
  586.0 0.9 sub.70
  586.9 84.4 %reduce-scatter.11.cloned.1.call-done = f32[128,256]{1,0:T(8,128)} async-done(((f32[4096,256]{1,0:T(8,128)}), f32[128,256]{1,0:T(8,128)}) %reduce-scatter.11.cloned.1.call-update) | async-done | bytes 131088 | tf_op jit(solution)/shard_map/reduce_scatter | solution.py:87
  671.3 0.9 sub.76
  672.2 0.7 pad_maximum_fusion.1
  672.9 4.1 all-to-all-start.2
  677.1 10.9 %fusion.23 = f32[1,512,256]{2,1,0:T(8,128)S(1)} fusion(f32[512,256]{1,0:T(8,128)S(1)} %convolution_multiply_fusion.2, f32[4096,256]{1,0:T(8,128)} %all-gather.12.cloned.1.call-done, f32[4096,512]{0,1:T(8,128)} %get-tuple-element.18, f32[4096]{0:T(1024)S(1)} %bitcast.84, f32[4096]{0:T(1024)S(1)} %get-tuple-element.7), kind=kOutput, calls=%fused_computation.25 | convolution fusion | flops 6448873472 | bytes 13664256 | tf_op jit(solution)/shard_map/dot_general | solution.py:11
  688.1 0.3 fusion.46
  688.4 0.9 convolution_negate_fusion
  689.3 1.0 pad_maximum_fusion
  690.4 140.6 %all-reduce.6.cloned.1.call-done = f32[64,256]{1,0:T(8,128)} async-done(((f32[64,256]{1,0:T(8,128)}), f32[64,256]{1,0:T(8,128)}) %all-reduce.6.cloned.1.call-update) | async-done | bytes 65552 | tf_op jit(solution)/shard_map/psum | solution.py:96
  831.0 1.5 copy.38
  (69 shorter events, 1.9 us)
Async XLA Ops:
  7.2 1.9 copy-start
  7.2 68.8 %all-gather.8.cloned.1.call-start = ((), (), s32[]{:S(2)}) async-start(), calls=%async_computation.7 | async-start | bytes 8650752 | tf_op jit(solution)/shard_map/all_gather | solution.py:58
  21.8 58.5 %copy-start.8 = (f32[2,512,256]{2,1,0:T(8,128)S(1)}, f32[2,512,256]{2,1,0:T(8,128)}, u32[]{:S(2)}) copy-start(f32[2,512,256]{2,1,0:T(8,128)} %param.7) | copy-start | bytes 3145732
  21.9 377.8 %reduce-scatter.5.cloned.1.call-start = ((), (), s32[]{:S(2)}) async-start(), calls=%async_computation.8 | async-start | bytes 4325376 | tf_op jit(solution)/shard_map/reduce_scatter | solution.py:72
  80.3 9.3 %copy-start.5 = (f32[1,128,32,256]{3,2,0,1:T(8,128)}, f32[1,128,32,256]{3,2,0,1:T(8,128)S(1)}, u32[]{:S(2)}) copy-start(f32[1,128,32,256]{3,2,0,1:T(8,128)S(1)} %get-tuple-element.14) | copy-start | bytes 12582916
  80.3 9.3 %copy-start.7 = (f32[1,128,32,256]{3,2,0,1:T(8,128)}, f32[1,128,32,256]{3,2,0,1:T(8,128)S(1)}, u32[]{:S(2)}) copy-start(f32[1,128,32,256]{3,2,0,1:T(8,128)S(1)} %get-tuple-element.13) | copy-start | bytes 12582916
  237.3 167.6 %reduce-scatter.9.cloned.1.call-start = ((), (), s32[]{:S(2)}) async-start(), calls=%async_computation.11 | async-start | bytes 4325376 | tf_op jit(solution)/shard_map/reduce_scatter | solution.py:72
  237.6 22.2 %copy-start.15 = (u32[128]{0:T(128)S(1)}, u32[128]{0:T(128)}, u32[]{:S(2)}) copy-start(u32[128]{0:T(128)} %constant.59) | copy-start | bytes 1540
  237.6 26.4 %copy-start.9 = (f32[2,4,32,256]{3,2,0,1:T(8,128)S(1)}, f32[2,4,32,256]{3,2,0,1:T(8,128)}, u32[]{:S(2)}) copy-start(f32[2,4,32,256]{3,2,0,1:T(8,128)} %all_to_all.15) | copy-start | bytes 786436
  255.7 8.3 all-to-all-start.1
  259.8 195.2 %all-gather.10.cloned.1.call-start = ((), (), s32[]{:S(2)}) async-start(), calls=%async_computation.9 | async-start | bytes 4325376 | tf_op jit(solution)/shard_map/all_gather | solution.py:79
  401.4 124.8 %all-gather.12.cloned.1.call-start = ((), (), s32[]{:S(2)}) async-start(), calls=%async_computation.12 | async-start | bytes 4325376 | tf_op jit(solution)/shard_map/all_gather | solution.py:79
  406.6 179.4 %reduce-scatter.7.cloned.1.call-start = ((), (), s32[]{:S(2)}) async-start(), calls=%async_computation.10 | async-start | bytes 4325376 | tf_op jit(solution)/shard_map/reduce_scatter | solution.py:87
  467.0 3.2 copy-start.2
  485.6 185.6 %reduce-scatter.11.cloned.1.call-start = ((), (), s32[]{:S(2)}) async-start(), calls=%async_computation.13 | async-start | bytes 4325376 | tf_op jit(solution)/shard_map/reduce_scatter | solution.py:87
  538.4 3.2 copy-start.3
  557.0 10.3 %copy-start.4 = (f32[4096,512]{0,1:T(8,128)S(1)}, f32[4096,512]{0,1:T(8,128)}, u32[]{:S(2)}) copy-start(f32[4096,512]{0,1:T(8,128)} %copy-done.3) | copy-start | bytes 25165828
  557.0 10.3 %copy-start.6 = (f32[1,128,32,256]{3,2,0,1:T(8,128)S(1)}, f32[1,128,32,256]{3,2,0,1:T(8,128)}, u32[]{:S(2)}) copy-start(f32[1,128,32,256]{3,2,0,1:T(8,128)} %copy-done.5) | copy-start | bytes 12582916
  557.0 17.1 %slice-start = ((s8[8388608]{0:T(1024)(128)(4,1)}), s8[4194304]{0:T(1024)(128)(4,1)S(1)}, s32[]{:S(2)}) async-start(s8[8388608]{0:T(1024)(128)(4,1)} %bitcast.73), calls=%async_computation.15 | async-start | bytes 8388608
  567.3 6.7 slice-start.1
  567.4 6.7 copy-start.14
  574.1 11.9 %copy-start.10 = (f32[128,256]{1,0:T(8,128)S(1)}, f32[128,256]{1,0:T(8,128)}, u32[]{:S(2)}) copy-start(f32[128,256]{1,0:T(8,128)} %get-tuple-element.10) | copy-start | bytes 393220
  574.1 97.2 %copy-start.11 = (f32[128,256]{1,0:T(8,128)S(1)}, f32[128,256]{1,0:T(8,128)}, u32[]{:S(2)}) copy-start(f32[128,256]{1,0:T(8,128)} %get-tuple-element.12) | copy-start | bytes 393220
  672.9 15.1 %all-to-all-start.2 = ((f32[2,4,32,256]{3,2,0,1:T(8,128)}), f32[2,4,32,256]{3,2,0,1:T(8,128)S(1)}, u32[]{:S(2)}, u32[]{:S(2)}) async-start(f32[2,4,32,256]{3,2,0,1:T(8,128)} %pad_maximum_fusion.1), calls=%async_computation.6 | async-start | bytes 524288 | tf_op jit(solution)/shard_map/all_to_all | solution.py:94
  677.1 11.3 %copy-start.13 = (s32[128]{0:T(128)S(1)}, s32[128]{0:T(128)}, u32[]{:S(2)}) copy-start(s32[128]{0:T(128)} %param.5) | copy-start | bytes 1540
  677.1 153.9 %all-reduce.6.cloned.1.call-start = ((), (), s32[]{:S(2)}) async-start(), calls=%async_computation.14 | async-start | bytes 131072 | tf_op jit(solution)/shard_map/psum | solution.py:96
  677.1 155.4 %copy-start.1 = (f32[64,256]{1,0:T(8,128)S(1)}, f32[64,256]{1,0:T(8,128)}, u32[]{:S(2)}) copy-start(f32[64,256]{1,0:T(8,128)} %param.6) | copy-start | bytes 196612
  688.4 144.1 %copy-start.12 = (f32[128,256]{1,0:T(8,128)}, f32[128,256]{1,0:T(8,128)S(1)}, u32[]{:S(2)}) copy-start(f32[128,256]{1,0:T(8,128)S(1)} %fusion.46) | copy-start | bytes 393220
Sparse Core Ops, SparseCore 0:
  22.0 53.9 all-gather.7
  237.5 82.1 reduce-scatter.4
  323.3 81.6 reduce-scatter.8
  407.6 47.2 all-gather.9
  457.6 45.2 all-gather.11
  506.4 79.4 reduce-scatter.6
  589.6 81.6 reduce-scatter.10
  689.5 141.5 all-reduce.5
where the time goes:
time: 847 us; the launch traced here: 840 us
  blocking collectives  342 us (40%)
  waiting for transfers between devices  294 us (35%)
  matrix products  146 us (17%)
  other arithmetic  18.8 us (2%)
  between operations  15.6 us (2%)
  local copies, waits for them, and re-layouts  14.2 us (2%)
  starting transfers between devices  8.75 us (1%)
    dot_general x16, matrix products, contract(): lax.dot_general(former, latter, (((former_dim,), (latter_dim,)), ((), ())...  146 us
    psum x1, waiting for transfers between devices, per_device(): lax.psum(-contract(onehot, item_grad, 0, 0), ('group', 'shard'))  141 us
    unnamed x1, blocking collectives  126 us
    pmax x1, blocking collectives, per_device(): peak_score = lax.pmax(jnp.max(scores, axis=1), 'shard')  121 us
    reduce_scatter x2, waiting for transfers between devices, per_device(): lax.psum_scatter(pushed, 'shard', scatter_dimension=0, tiled=True)  88.1 us
    all_gather x1, waiting for transfers between devices, per_device(): lax.all_gather(arrived, 'shard', axis=1, tiled=True)  54.1 us
    all_gather x2, blocking collectives, per_device(): lax.all_gather(denominator_own, 'shard', axis=0, tiled=True)  43.2 us
    all_gather x2, blocking collectives, per_device(): lax.all_gather(own_inner, 'shard', axis=0, tiled=True)  40.5 us
  transfers between devices with their start and end apart: 10, of which 7 were waited for; matrix products, arithmetic and copies ran while one was open for 15% of the time, Pallas kernels for 0%

commit v1 on v0

--- a/solution.py
+++ b/solution.py
@@ -93,7 +93,9 @@
     returned = jnp.stack(row_grads).reshape(local_groups, group_count, slot_size, feature_count)
     homeward = lax.all_to_all(returned, "group", split_axis=1, concat_axis=1, tiled=True)
     item_grad = contract(placing, homeward.reshape(slot_total, feature_count), 0, 0)
-    coarse_grad = lax.psum(-contract(onehot, item_grad, 0, 0), ("group", "shard"))
+    coarse_grad = jnp.sum(
+        lax.all_gather(-contract(onehot, item_grad, 0, 0), ("group", "shard")), axis=0
+    )
     return (item_grad, fine_grad, coarse_grad)
 
 

time: 847 us -> 773 us (0.913)
  waiting for transfers between devices: 294 us -> 213 us
  blocking collectives: 342 us -> 352 us
    psum x1 -> x0, waiting for transfers between devices: 141 us -> none  [per_device(): lax.psum(-contract(onehot, item_grad, 0, 0), ('group', 'shard'))]
    all_gather x0 -> x1, waiting for transfers between devices: none -> 33.8 us  [per_device(): lax.all_gather(-contract(onehot, item_grad, 0, 0), ('group', 'shard'))]
    reduce_scatter x2, waiting for transfers between devices: 88.1 us -> 113 us  [per_device(): lax.psum_scatter(pushed, 'shard', scatter_dimension=0, tiled=True)]
    all_to_all x0 -> x1, blocking collectives: none -> 9.63 us  [per_device(): lax.all_to_all(returned, 'group', split_axis=1, concat_axis=1, tiled=True)]
  transfers between devices with their start and end apart: 10 -> 9, of which waited for: 7 -> 7; matrix products, arithmetic and copies ran while one was open for 15% -> 16% of each run, Pallas kernels for 0% -> 0%
where the time goes in v1:
time: 773 us; the launch traced here: 766 us
  blocking collectives  352 us (46%)
  waiting for transfers between devices  213 us (28%)
  matrix products  146 us (19%)
  other arithmetic  22.6 us (3%)
  between operations  15.4 us (2%)
  local copies, waits for them, and re-layouts  12.7 us (2%)
    dot_general x16, matrix products, contract(): lax.dot_general(former, latter, (((former_dim,), (latter_dim,)), ((), ())...  146 us
    unnamed x1, blocking collectives  126 us
    pmax x1, blocking collectives, per_device(): peak_score = lax.pmax(jnp.max(scores, axis=1), 'shard')  122 us
    reduce_scatter x2, waiting for transfers between devices, per_device(): lax.psum_scatter(pushed, 'shard', scatter_dimension=0, tiled=True)  113 us
    all_gather x1, waiting for transfers between devices, per_device(): lax.all_gather(arrived, 'shard', axis=1, tiled=True)  54.1 us
    all_gather x2, blocking collectives, per_device(): lax.all_gather(denominator_own, 'shard', axis=0, tiled=True)  43.2 us
    all_gather x2, blocking collectives, per_device(): lax.all_gather(own_inner, 'shard', axis=0, tiled=True)  40.5 us
    all_gather x1, waiting for transfers between devices, per_device(): lax.all_gather(-contract(onehot, item_grad, 0, 0), ('group', 'shard'))  33.8 us
  transfers between devices with their start and end apart: 9, of which 7 were waited for; matrix products, arithmetic and copies ran while one was open for 16% of the time, Pallas kernels for 0%

profile of v1, /device:TPU:1, one launch (start us, length us, event | category | flops | bytes accessed | tf_op | source)
XLA Modules:
  0.0 766.0 jit_solution(13480117153895938123)
XLA Ops:
  7.2 0.7 and_select_fusion.2
  8.3 0.7 multiply_add_fusion
  9.0 1.2 convolution_subtract_fusion
  10.2 0.3 fusion.47
  10.5 11.3 %all_to_all.15 = f32[2,4,32,256]{3,2,0,1:T(8,128)} all-to-all(f32[2,4,32,256]{3,2,0,1:T(8,128)S(1)} %copy.28), channel_id=1, replica_groups=mesh['group'=4,'shard'=32] {'group'}, dimensions={1} | all-to-all | bytes 524288 | tf_op jit(solution)/shard_map/all_to_all | solution.py:49
  21.9 54.1 %all-gather.10.cloned.1.call-done = f32[2,128,32,256]{3,2,0,1:T(8,128)} async-done(((f32[2,4,32,256]{3,2,0,1:T(8,128)}), f32[2,128,32,256]{3,2,0,1:T(8,128)}) %all-gather.10.cloned.1.call-update) | async-done | bytes 8388624 | tf_op jit(solution)/shard_map/all_gather | solution.py:58
  76.0 4.4 fusion.61
  80.4 9.3 %multiply_reduce_fusion = (f32[4096]{0:T(1024)S(1)}, f32[4096,512]{0,1:T(8,128)}) fusion(f32[4096,256]{1,0:T(8,128)S(1)} %bitcast.78, f32[2,512,256]{2,1,0:T(8,128)S(1)} %copy-done.7), kind=kOutput, calls=%fused_computation.4 | convolution fusion | flops 6446641152 | bytes 13123584 | tf_op jit(solution)/shard_map/dot_general | solution.py:11
  89.6 9.2 %multiply_reduce_fusion.1 = (f32[4096]{0:T(1024)S(1)}, f32[4096,512]{0,1:T(8,128)}) fusion(f32[4096,256]{1,0:T(8,128)S(1)} %bitcast.80, f32[2,512,256]{2,1,0:T(8,128)S(1)} %copy-done.7), kind=kOutput, calls=%fused_computation.5 | convolution fusion | flops 6446641152 | bytes 13123584 | tf_op jit(solution)/shard_map/dot_general | solution.py:11
  98.8 121.7 %all-reduce.3 = (f32[4096]{0:T(1024)S(1)}, f32[4096]{0:T(1024)S(1)}) all-reduce(f32[4096]{0:T(1024)S(1)} %get-tuple-element.17, f32[4096]{0:T(1024)S(1)} %get-tuple-element.19), channel_id=1, replica_groups=mesh['group'=4,'shard'=32] {'shard'}, use_global_device_ids=true, to_apply=%region_11.12 | all-reduce | flops 8192 | bytes 65536 | tf_op jit(solution)/shard_map/pmax | solution.py:67
  220.5 17.2 %fusion = f32[4096,256]{1,0:T(8,128)} fusion(f32[4096,512]{0,1:T(8,128)} %get-tuple-element.20, f32[4096]{0:T(1024)S(1)} %get-tuple-element.8, f32[2,512,256]{2,1,0:T(8,128)S(1)} %copy-done.7), kind=kOutput, calls=%fused_computation.8 | convolution fusion | flops 6446645248 | bytes 13123584 | tf_op jit(solution)/shard_map/dot_general | solution.py:11
  237.7 0.2 reduce-scatter.9.cloned.1.call-start
  238.0 17.2 %fusion.3 = f32[4096,256]{1,0:T(8,128)} fusion(f32[4096,512]{0,1:T(8,128)} %get-tuple-element.18, f32[4096]{0:T(1024)S(1)} %get-tuple-element.7, f32[2,512,256]{2,1,0:T(8,128)S(1)} %copy-done.7), kind=kOutput, calls=%fused_computation.11 | convolution fusion | flops 6446645248 | bytes 13123584 | tf_op jit(solution)/shard_map/dot_general | solution.py:11
  255.4 0.6 copy.29
  256.0 4.1 all-to-all-start.1
  260.2 0.6 dynamic-slice
  261.4 2.9 all-to-all-done.1
  264.4 5.0 fusion.2
  269.4 5.0 fusion.5
  274.4 125.5 %all-reduce.2 = (f32[4096]{0:T(1024)S(1)}, f32[4096]{0:T(1024)S(1)}) all-reduce(f32[4096]{0:T(1024)S(1)} %fusion.5, f32[4096]{0:T(1024)S(1)} %fusion.2), channel_id=6, replica_groups=mesh['group'=4,'shard'=32] {'shard'}, use_global_device_ids=true, to_apply=%region_13.14.clone | all-reduce | flops 8192 | bytes 65536
  400.0 1.7 multiply_reduce_fusion.3
  401.9 3.5 reduce-scatter.9.cloned.1.call-done
  405.4 1.7 multiply_reduce_fusion.2
  407.2 22.6 %all-gather.1 = f32[32,1,128]{2,1,0:T(1,128)S(1)} all-gather(f32[1,1,128]{2,1,0:T(1,128)S(1)} %dynamic-slice_bitcast_fusion), channel_id=1, replica_groups=mesh['group'=4,'shard'=32] {'shard'}, dimensions={0}, use_global_device_ids=true | all-gather | bytes 16896 | tf_op jit(solution)/shard_map/all_gather | solution.py:81
  429.7 20.6 %all-gather.2 = f32[32,1,128]{2,1,0:T(1,128)S(1)} all-gather(f32[1,1,128]{2,1,0:T(1,128)S(1)} %bitcast.93), channel_id=1, replica_groups=mesh['group'=4,'shard'=32] {'shard'}, dimensions={0}, use_global_device_ids=true | all-gather | bytes 16896 | tf_op jit(solution)/shard_map/all_gather | solution.py:80
  450.3 5.1 all-gather.12.cloned.1.call-done
  455.4 12.0 %subtract_multiply_fusion.1 = f32[4096,512]{0,1:T(8,128)S(1)} fusion(f32[4096,256]{1,0:T(8,128)} %all-gather.12.cloned.1.call-done, f32[4096]{0:T(1024)S(1)} %bitcast.91, f32[4096]{0:T(1024)S(1)} %bitcast.87, f32[4096]{0:T(1024)S(1)} %get-tuple-element.8, f32[4096,512]{0,1:T(8,128)} %get-tuple-element.20, f32[2,512,256]{2,1,0:T(8,128)S(1)} %copy-done.7), kind=kOutput, calls=%fused_computation.2 | convolution fusion | flops 6452936704 | bytes 21544960 | tf_op jit(solution)/shard_map/dot_general | solution.py:11
  467.4 3.2 copy-done.2
  470.6 15.4 %convolution_multiply_fusion.1 = f32[4096,256]{1,0:T(8,128)} fusion(f32[4096,512]{0,1:T(8,128)S(1)} %subtract_multiply_fusion.1, f32[2,512,256]{2,1,0:T(8,128)S(1)} %copy-done.7), kind=kOutput, calls=%fused_computation.7 | convolution fusion | flops 6443499520 | bytes 13107200 | tf_op jit(solution)/shard_map/dot_general | solution.py:11
  486.2 20.7 %all-gather.3 = f32[32,1,128]{2,1,0:T(1,128)S(1)} all-gather(f32[1,1,128]{2,1,0:T(1,128)S(1)} %dynamic-slice_bitcast_fusion.1), channel_id=1, replica_groups=mesh['group'=4,'shard'=32] {'shard'}, dimensions={0}, use_global_device_ids=true | all-gather | bytes 16896 | tf_op jit(solution)/shard_map/all_gather | solution.py:81
  506.9 20.0 %all-gather.4 = f32[32,1,128]{2,1,0:T(1,128)S(1)} all-gather(f32[1,1,128]{2,1,0:T(1,128)S(1)} %bitcast.94), channel_id=1, replica_groups=mesh['group'=4,'shard'=32] {'shard'}, dimensions={0}, use_global_device_ids=true | all-gather | bytes 16896 | tf_op jit(solution)/shard_map/all_gather | solution.py:80
  526.9 12.2 %subtract_multiply_fusion = f32[4096,512]{0,1:T(8,128)S(1)} fusion(f32[4096,256]{1,0:T(8,128)} %all-gather.14.cloned.1.call-done, f32[4096]{0:T(1024)S(1)} %bitcast.92, f32[4096]{0:T(1024)S(1)} %bitcast.89, f32[4096]{0:T(1024)S(1)} %get-tuple-element.7, f32[4096,512]{0,1:T(8,128)} %get-tuple-element.18, f32[2,512,256]{2,1,0:T(8,128)S(1)} %copy-done.7), kind=kOutput, calls=%fused_computation | convolution fusion | flops 6452936704 | bytes 21544960 | tf_op jit(solution)/shard_map/dot_general | solution.py:11
  539.1 3.2 copy-done.3
  542.3 15.4 %convolution_multiply_fusion = f32[4096,256]{1,0:T(8,128)} fusion(f32[4096,512]{0,1:T(8,128)S(1)} %subtract_multiply_fusion, f32[2,512,256]{2,1,0:T(8,128)S(1)} %copy-done.7), kind=kOutput, calls=%fused_computation.6 | convolution fusion | flops 6443499520 | bytes 13107200 | tf_op jit(solution)/shard_map/dot_general | solution.py:11
  557.8 28.7 %reduce-scatter.7.cloned.1.call-done = f32[128,256]{1,0:T(8,128)} async-done(((f32[4096,256]{1,0:T(8,128)}), f32[128,256]{1,0:T(8,128)}) %reduce-scatter.7.cloned.1.call-update) | async-done | bytes 131088 | tf_op jit(solution)/shard_map/reduce_scatter | solution.py:87
  586.4 0.9 sub.70
  587.4 84.4 %reduce-scatter.11.cloned.1.call-done = f32[128,256]{1,0:T(8,128)} async-done(((f32[4096,256]{1,0:T(8,128)}), f32[128,256]{1,0:T(8,128)}) %reduce-scatter.11.cloned.1.call-update) | async-done | bytes 131088 | tf_op jit(solution)/shard_map/reduce_scatter | solution.py:87
  671.8 0.9 sub.76
  672.7 9.6 %all_to_all.16 = f32[2,4,32,256]{3,2,0,1:T(8,128)S(1)} all-to-all(f32[2,4,32,256]{3,2,0,1:T(8,128)S(1)} %pad_maximum_fusion.1), channel_id=1, replica_groups=mesh['group'=4,'shard'=32] {'group'}, dimensions={1} | all-to-all | bytes 524288 | tf_op jit(solution)/shard_map/all_to_all | solution.py:94
  682.4 0.3 fusion.46
  682.7 0.9 convolution_negate_fusion
  683.7 10.0 %convolution_multiply_fusion.3 = f32[512,256]{1,0:T(8,128)S(1)} fusion(f32[4096,512]{0,1:T(8,128)} %copy-done.2, f32[4096,256]{1,0:T(8,128)} %bitcast.81), kind=kOutput, calls=%fused_computation.21 | convolution fusion | flops 6442582016 | bytes 13107200 | tf_op jit(solution)/shard_map/dot_general | solution.py:11
  693.7 9.9 %convolution_multiply_fusion.2 = f32[512,256]{1,0:T(8,128)S(1)} fusion(f32[4096,512]{0,1:T(8,128)} %copy-done.3, f32[4096,256]{1,0:T(8,128)S(1)} %bitcast.79), kind=kOutput, calls=%fused_computation.20 | convolution fusion | flops 6442582016 | bytes 13107200 | tf_op jit(solution)/shard_map/dot_general | solution.py:11
  703.7 7.8 %fusion.17 = f32[1,512,256]{2,1,0:T(8,128)S(1)} fusion(f32[512,256]{1,0:T(8,128)S(1)} %convolution_multiply_fusion.3, f32[4096,256]{1,0:T(8,128)S(1)} %copy-done.13, f32[4096,512]{0,1:T(8,128)S(1)} %bitcast.77, f32[4096]{0:T(1024)S(1)} %bitcast.88, f32[4096]{0:T(1024)S(1)} %get-tuple-element.8), kind=kOutput, calls=%fused_computation.23 | convolution fusion | flops 6448873472 | bytes 13664256 | tf_op jit(solution)/shard_map/dot_general | solution.py:11
  711.6 8.1 %fusion.23 = f32[1,512,256]{2,1,0:T(8,128)S(1)} fusion(f32[512,256]{1,0:T(8,128)S(1)} %convolution_multiply_fusion.2, f32[4096,256]{1,0:T(8,128)S(1)} %copy-done.14, f32[4096,512]{0,1:T(8,128)S(1)} %bitcast.75, f32[4096]{0:T(1024)S(1)} %bitcast.90, f32[4096]{0:T(1024)S(1)} %get-tuple-element.7), kind=kOutput, calls=%fused_computation.25 | convolution fusion | flops 6448873472 | bytes 13664256 | tf_op jit(solution)/shard_map/dot_general | solution.py:11
  719.7 1.0 pad_maximum_fusion
  720.7 33.8 %all-gather.16.cloned.1.call-done = f32[8192,256]{1,0:T(8,128)} async-done(((f32[64,256]{1,0:T(8,128)}), f32[8192,256]{1,0:T(8,128)}) %all-gather.16.cloned.1.call-update) | async-done | bytes 8388624 | tf_op jit(solution)/shard_map/all_gather | solution.py:97
  754.5 4.5 reduce_sum.69
  (73 shorter events, 1.7 us)
Async XLA Ops:
  7.2 1.9 copy-start
  7.2 68.8 %all-gather.10.cloned.1.call-start = ((), (), s32[]{:S(2)}) async-start(), calls=%async_computation.7 | async-start | bytes 8650752 | tf_op jit(solution)/shard_map/all_gather | solution.py:58
  21.8 58.5 %copy-start.7 = (f32[2,512,256]{2,1,0:T(8,128)S(1)}, f32[2,512,256]{2,1,0:T(8,128)}, u32[]{:S(2)}) copy-start(f32[2,512,256]{2,1,0:T(8,128)} %param.7) | copy-start | bytes 3145732
  21.8 378.2 %reduce-scatter.5.cloned.1.call-start = ((), (), s32[]{:S(2)}) async-start(), calls=%async_computation.8 | async-start | bytes 4325376 | tf_op jit(solution)/shard_map/reduce_scatter | solution.py:72
  80.3 9.3 %copy-start.4 = (f32[1,128,32,256]{3,2,0,1:T(8,128)}, f32[1,128,32,256]{3,2,0,1:T(8,128)S(1)}, u32[]{:S(2)}) copy-start(f32[1,128,32,256]{3,2,0,1:T(8,128)S(1)} %get-tuple-element.14) | copy-start | bytes 12582916
  80.3 9.3 %copy-start.6 = (f32[1,128,32,256]{3,2,0,1:T(8,128)}, f32[1,128,32,256]{3,2,0,1:T(8,128)S(1)}, u32[]{:S(2)}) copy-start(f32[1,128,32,256]{3,2,0,1:T(8,128)S(1)} %get-tuple-element.13) | copy-start | bytes 12582916
  237.7 167.6 %reduce-scatter.9.cloned.1.call-start = ((), (), s32[]{:S(2)}) async-start(), calls=%async_computation.11 | async-start | bytes 4325376 | tf_op jit(solution)/shard_map/reduce_scatter | solution.py:72
  238.0 22.2 %copy-start.15 = (u32[128]{0:T(128)S(1)}, u32[128]{0:T(128)}, u32[]{:S(2)}) copy-start(u32[128]{0:T(128)} %constant.59) | copy-start | bytes 1540
  238.0 26.4 %copy-start.8 = (f32[2,4,32,256]{3,2,0,1:T(8,128)S(1)}, f32[2,4,32,256]{3,2,0,1:T(8,128)}, u32[]{:S(2)}) copy-start(f32[2,4,32,256]{3,2,0,1:T(8,128)} %all_to_all.15) | copy-start | bytes 786436
  256.0 8.3 %all-to-all-start.1 = ((f32[2,4,32]{2,0,1:T(2,128)}), f32[2,4,32]{2,0,1:T(2,128)S(1)}, u32[]{:S(2)}, u32[]{:S(2)}) async-start(f32[2,4,32]{2,0,1:T(2,128)} %copy.29), calls=%async_computation.2 | async-start | bytes 8192 | tf_op jit(solution)/shard_map/all_to_all | solution.py:50
  260.2 195.2 %all-gather.12.cloned.1.call-start = ((), (), s32[]{:S(2)}) async-start(), calls=%async_computation.9 | async-start | bytes 4325376 | tf_op jit(solution)/shard_map/all_gather | solution.py:79
  401.7 125.2 %all-gather.14.cloned.1.call-start = ((), (), s32[]{:S(2)}) async-start(), calls=%async_computation.12 | async-start | bytes 4325376 | tf_op jit(solution)/shard_map/all_gather | solution.py:79
  407.1 179.4 %reduce-scatter.7.cloned.1.call-start = ((), (), s32[]{:S(2)}) async-start(), calls=%async_computation.10 | async-start | bytes 4325376 | tf_op jit(solution)/shard_map/reduce_scatter | solution.py:87
  467.4 3.2 copy-start.2
  486.1 185.7 %reduce-scatter.11.cloned.1.call-start = ((), (), s32[]{:S(2)}) async-start(), calls=%async_computation.13 | async-start | bytes 4325376 | tf_op jit(solution)/shard_map/reduce_scatter | solution.py:87
  539.1 3.2 copy-start.3
  542.3 44.2 %copy-start.9 = (f32[128,256]{1,0:T(8,128)S(1)}, f32[128,256]{1,0:T(8,128)}, u32[]{:S(2)}) copy-start(f32[128,256]{1,0:T(8,128)} %get-tuple-element.10) | copy-start | bytes 393220
  542.3 129.5 %copy-start.10 = (f32[128,256]{1,0:T(8,128)S(1)}, f32[128,256]{1,0:T(8,128)}, u32[]{:S(2)}) copy-start(f32[128,256]{1,0:T(8,128)} %get-tuple-element.12) | copy-start | bytes 393220
  542.3 140.4 %copy-start.12 = (s32[128]{0:T(128)S(1)}, s32[128]{0:T(128)}, u32[]{:S(2)}) copy-start(s32[128]{0:T(128)} %param.5) | copy-start | bytes 1540
  557.7 196.8 %all-gather.16.cloned.1.call-start = ((), (), s32[]{:S(2)}) async-start(), calls=%async_computation.14 | async-start | bytes 8454144 | tf_op jit(solution)/shard_map/all_gather | solution.py:97
  682.7 11.0 %copy-start.11 = (f32[128,256]{1,0:T(8,128)}, f32[128,256]{1,0:T(8,128)S(1)}, u32[]{:S(2)}) copy-start(f32[128,256]{1,0:T(8,128)S(1)} %fusion.46) | copy-start | bytes 393220
  683.7 10.0 %copy-start.5 = (f32[1,128,32,256]{3,2,0,1:T(8,128)S(1)}, f32[1,128,32,256]{3,2,0,1:T(8,128)}, u32[]{:S(2)}) copy-start(f32[1,128,32,256]{3,2,0,1:T(8,128)} %copy-done.4) | copy-start | bytes 12582916
  683.7 20.0 %slice-start.2 = ((s8[8388608]{0:T(1024)(128)(4,1)}), s8[4194304]{0:T(1024)(128)(4,1)S(1)}, s32[]{:S(2)}) async-start(s8[8388608]{0:T(1024)(128)(4,1)} %bitcast.76), calls=%async_computation.17 | async-start | bytes 8388608
  693.7 10.0 %slice-start.3 = ((s8[8388608]{0:T(1024)(128)(4,1)}), s8[4194304]{0:T(1024)(128)(4,1)S(1)}, s32[]{:S(2)}) async-start(s8[8388608]{0:T(1024)(128)(4,1)} %bitcast.76), calls=%async_computation.18 | async-start | bytes 8388608
  693.7 10.0 %copy-start.13 = (f32[4096,256]{1,0:T(8,128)S(1)}, f32[4096,256]{1,0:T(8,128)}, u32[]{:S(2)}) copy-start(f32[4096,256]{1,0:T(8,128)} %all-gather.12.cloned.1.call-done) | copy-start | bytes 12582916
  693.7 17.8 %slice-start = ((s8[8388608]{0:T(1024)(128)(4,1)}), s8[4194304]{0:T(1024)(128)(4,1)S(1)}, s32[]{:S(2)}) async-start(s8[8388608]{0:T(1024)(128)(4,1)} %bitcast.74), calls=%async_computation.15 | async-start | bytes 8388608
  703.7 7.8 %slice-start.1 = ((s8[8388608]{0:T(1024)(128)(4,1)}), s8[4194304]{0:T(1024)(128)(4,1)S(1)}, s32[]{:S(2)}) async-start(s8[8388608]{0:T(1024)(128)(4,1)} %bitcast.74), calls=%async_computation.16 | async-start | bytes 8388608
  703.7 7.8 %copy-start.14 = (f32[4096,256]{1,0:T(8,128)S(1)}, f32[4096,256]{1,0:T(8,128)}, u32[]{:S(2)}) copy-start(f32[4096,256]{1,0:T(8,128)} %all-gather.14.cloned.1.call-done) | copy-start | bytes 12582916
  711.6 47.4 %copy-start.1 = (f32[64,256]{1,0:T(8,128)S(1)}, f32[64,256]{1,0:T(8,128)}, u32[]{:S(2)}) copy-start(f32[64,256]{1,0:T(8,128)} %param.6) | copy-start | bytes 196612
Sparse Core Ops, SparseCore 0:
  22.0 53.9 all-gather.9
  237.9 82.1 reduce-scatter.4
  323.7 81.6 reduce-scatter.8
  408.1 47.2 all-gather.11
  458.1 45.2 all-gather.13
  506.9 79.5 reduce-scatter.6
  590.1 81.6 reduce-scatter.10
  683.8 70.6 all-gather.15
